TPU v7x, 32 devices: a whole 2x2x4 slice. The times are simulated.
32 devices in a mesh: groups: 2 (over y), lon: 4 (over z), lat: 2 (over x), sub: 2 (over core).
Axes of the slice: x: 2, y: 2, z: 4, core: 2. Of those that a mesh axis runs over, the one named last changes fastest.
Arguments:
- tokens: bfloat16 [512, 200, 384], P(('groups', 'lat', 'lon')), parts along dimension 0, may hold values from -130 to 130, as said below
- land_bits: int32 [512, 200], P(('groups', 'lat', 'lon')), parts along dimension 0, may hold values from 0 to 1, as said below
- ocean_list: int32 [4, 128], P(('groups', 'lat')), parts along dimension 0, may hold values from 0 to 128, as said below
- w_qkv: bfloat16 [2, 3, 384, 384], P(None, None, None, 'sub'), as said below
- w_out: bfloat16 [2, 384, 384], P(None, 'sub'), may hold values from -0.3125 to 0.3125
Outputs:
- advanced: bfloat16 [512, 200, 384], P(('groups', 'lat', 'lon')), parts along dimension 0
There are 2 independent parts, one for each index of `groups`. A program takes and returns all parts, laid end to end along the dimension named above; an argument that names none is the same for every part. Nothing has to cross between parts.
Inputs may be any that keep to these rules, and one draw needn't show every extreme that they name: `ocean_list`: each row lists its band's ocean windows in increasing order and then holds 128. A row lists at least 72 and at most 96 windows; some row lists exactly 96. In each window row of a band the listed windows form one run along longitude, which may wrap around. `land_bits`: every token of a window that its band's row of ocean_list does not list is land; in listed windows about a quarter of the tokens are land. `tokens`: finite values. `w_qkv`: entries lie within 165 / sqrt(384) in magnitude.
All inputs are finite; a program needn't handle non-finite values.
Results may differ from a plain program's by a relative error of at most 0.013.
Values may be sent and summed in bfloat16 or wider, within the bound.
No kernel may reach another device: no remote copies, remote signals or barrier semaphores. Data moves between devices by JAX's collectives and lax.ppermute only.
A program may use at most 64 MiB of HBM per device.

v0:
```python
import functools

import jax
import jax.numpy as jnp
import numpy as np
from jax import lax
from jax.experimental import pallas as pl
from jax.experimental.pallas import tpu as pltpu
from jax.sharding import PartitionSpec as P


HD = 32
WH = 10
WW = 20
T = WH * WW
ROWS = 4
TP = 208
KP = 256
LIMIT = 20
BRING = 48
REC = 224
HALF = 112
SENT = HALF + 16
NEG = -1e30
SCALE = HD**-0.5 * 1.4426950408889634
f32 = jnp.float32
bf16 = jnp.bfloat16
NT = (((1,), (1,)), ((), ()))
HBM = pl.BlockSpec(memory_space=pltpu.HBM)
ANY = pl.BlockSpec(memory_space=pl.ANY)
VMEM = pl.BlockSpec(memory_space=pltpu.VMEM)


def normed(x):
    centred = x - jnp.mean(x, axis=-1, keepdims=True)
    variance = jnp.mean(centred * centred, axis=-1, keepdims=True)
    return (centred * lax.rsqrt(variance + 1e-05)).astype(bf16)


def blocks(pairs, load, again, land_rows, keeps, put, weights, slots, heads=4, ahead=1):
    wqk, wv, wout = weights
    d = wv.shape[0]
    lane = lax.broadcasted_iota(jnp.int32, (1, 128), 1)
    masks = [jnp.where((lane >= HD * j) & (lane < HD * j + HD), 1.0, 0.0).astype(bf16) for j in range(4)]
    unit = jnp.broadcast_to(jnp.where(lane == 0, 1.0, 0.0), (TP, 128)).astype(bf16)
    ones = jnp.ones((16, TP), bf16)
    total = len(pairs)

    def before(t):
        norm, qk, values, _, _, bias, land = slots[t % 2]

        def normal(i):
            norm[i * TP : i * TP + T, :] = normed(load(t, i))

        def mask():
            rows = land_rows(t)
            land[...] = jnp.transpose(jnp.concatenate(rows + [rows[0]] * 6, axis=0))
            for i in range(2):
                bias[i] = jnp.where(lane == 0, land[:TP, i : i + 1] * NEG, 0.0).astype(bf16)

        def project(at):
            wide = lax.broadcasted_iota(jnp.int32, (1, 256), 1) + at
            got = lax.dot_general(norm[...], wqk[at : at + 256], NT, preferred_element_type=f32)
            qk[:, at : at + 256] = (got * jnp.where(wide < d, SCALE, 1.0)).astype(bf16)

        def value(i):
            got = lax.dot_general(wv[...], norm[i * TP : i * TP + TP], NT, preferred_element_type=f32)
            values[i] = got.astype(bf16)

        return (
            [functools.partial(normal, i) for i in range(2)] + [mask]
            + [functools.partial(project, at) for at in range(0, 2 * d, 256)]
            + [functools.partial(value, i) for i in range(2)]
        )

    def after(t):
        _, _, _, mixed, joined, _, land = slots[t % 2]
        held = {}

        def turn(i):
            joined[i * TP : i * TP + TP] = jnp.transpose(mixed[i])

        def out():
            held["update"] = jnp.dot(joined[...], wout[...], preferred_element_type=f32)

        def add(i):
            keep = (1.0 - land[:T, i : i + 1]) * keeps(t, i)
            put(t, i, (again(t, i) + held["update"][i * TP : i * TP + T] * keep).astype(bf16))

        return [functools.partial(turn, i) for i in range(2)] + [out] + [functools.partial(add, i) for i in range(2)]

    units = [
        (t, i, g, tuple(range(a, a + heads)))
        for t in range(total) for i in range(2) for g in range(d // 128) for a in range(0, 4, heads)
    ]
    per = len(units) // total
    scores, probs = {}, {}

    def score(u):
        t, i, g, hs = units[u]
        qk, bias = slots[t % 2][1], slots[t % 2][5]
        k = qk[i * TP : i * TP + TP, d + 128 * g : d + 128 * g + 128]
        q = jnp.concatenate([qk[i * TP : i * TP + TP, 128 * g : 128 * g + 128], unit], axis=1)
        b = bias[i]
        keyed = jnp.concatenate([jnp.concatenate([k * masks[j], b], axis=1) for j in hs], axis=0)
        got = lax.dot_general(keyed, q, NT, preferred_element_type=f32)
        scores[u] = [got[n * TP : n * TP + TP] for n in range(len(hs))]

    def soften(u):
        probs[u] = [
            jnp.exp2((s - jnp.max(s, axis=0, keepdims=True)).astype(bf16)) for s in scores.pop(u)
        ]

    def mix(u):
        t, i, g, hs = units[u]
        values, mixed = slots[t % 2][2], slots[t % 2][3]
        for j, p in zip(hs, probs.pop(u)):
            at = 128 * g + HD * j
            both = jnp.dot(
                jnp.concatenate([values[i, at : at + HD], ones], axis=0), p, preferred_element_type=f32
            )
            mixed[i, at : at + HD] = (both[:HD] * (1.0 / both[HD : HD + 1])).astype(bf16)

    for piece in before(0):
        piece()
    pieces, step, place = [], 1.0, 1
    for k in range(len(units) + 2 * ahead):
        t, at = k // per, k % per
        if at == 2 * ahead:
            pieces = (after(t - 1) if t else []) + (before(t + 1) if t + 1 < total else [])
            step, place = (per - 2 * ahead) / (len(pieces) + 1), 1
        if k < len(units):
            score(k)
        if 0 <= k - ahead < len(units):
            soften(k - ahead)
        if 0 <= k - 2 * ahead:
            mix(k - 2 * ahead)
        while pieces and (at == per - 1 or at - 2 * ahead + 1 >= place * step):
            pieces.pop(0)()
            place += 1
    for piece in pieces + after(total - 1):
        piece()


def paired(windows):
    padded = list(windows) + [windows[-1]] * (len(windows) % 2)
    return [padded[n : n + 2] for n in range(0, len(padded), 2)]


def join_weights(block, sources, weights):
    wqk, wv, wout = weights
    for n in range(2):
        qkv, out = sources[2 * n : 2 * n + 2]
        half = out.shape[1]
        rows = slice(n * half, n * half + half)
        for part in range(2):
            wqk[part * 2 * half + n * half : part * 2 * half + n * half + half] = qkv[block, part]
        wv[rows] = qkv[block, 2]
        wout[rows] = out[block]


def clear_pads(slots):
    for slot in slots:
        for i in range(2):
            slot[0][i * TP + TP - 16 : i * TP + TP, :] = jnp.zeros((16, slot[0].shape[1]), bf16)


LOW = T - HALF + 8
MID = T // 2 // 16 * 16


def side_masks(left):
    token = lax.broadcasted_iota(jnp.int32, left.shape, 0)
    left[...] = jnp.where(token % WW < WW // 2, 1.0, 0.0).astype(bf16)


def merged(at, left, d):
    def pick(below, lo, hi):
        side = jnp.concatenate([left[lo:hi]] * (d // 128), axis=1) > 0.5
        return jnp.where(side, at(1, below, slice(lo, hi)), at(0, below, slice(lo, hi)))

    row = lax.broadcasted_iota(jnp.int32, (HALF - MID, d), 0) + MID
    middle = jnp.where(row < T // 2, pick(1, MID, HALF).astype(f32), pick(0, MID, HALF).astype(f32)).astype(bf16)
    return jnp.concatenate([pick(1, 0, MID), middle, pick(0, HALF, T)], axis=0)


class Plan:
    def __init__(self, columns, bands):
        self.c = c = columns
        self.low = low = (c + 1) // 2
        self.up = c > low
        last = ROWS - 1
        sent = [(0, r) for r in range(ROWS)]
        sent += [(x, 0) for x in range(1, min(low, c - 1) + 1)]
        sent += [(x, last) for x in range(max(low, 1), c)]
        self.first_a = sent
        self.first_b = [(x, r) for x in range(c) for r in range(ROWS) if (x, r) not in sent]
        self.to_left = [(0, r) for r in range(ROWS)]
        self.to_above = [(x, 0) for x in range(min(low, c - 1) + 1)]
        self.to_below = [(x, last) for x in range(low, c)]
        self.to_diag = (0, last) if self.up else (0, 0)
        self.rim = [(c - 1, r) for r in range(last)]
        self.lower = [(x, last) for x in range(low)]
        self.upper = [(x, -1) for x in range(low, c)]
        self.inner = [(x, r) for x in range(c - 1) for r in range(last)]
        self.extra = len(self.rim) % 2 if self.inner else 0
        self.some = self.rim + self.inner[: self.extra]
        self.rest = self.inner[self.extra :]
        self.joined = self.up and bands == 2
        self.back_right = [(c - 1, r) for r in (range(-1, last) if self.up else range(ROWS))]

    def index(self, window):
        return window[0] * ROWS + window[1]


def bring_kernel(plan, tokens, land, ocean, qkv, out, mine, sem):
    start = lax.axis_index("sub") * (plan.c * ROWS)
    copy = pltpu.make_async_copy(tokens.at[pl.ds(start, plan.c * ROWS)], mine, sem)
    copy.start()
    copy.wait()


def first_kernel(plan, which, *refs):
    windows = plan.first_b if which else plan.first_a
    tokens, land, ocean = refs[:3]
    sources, refs = refs[3:7], refs[7:]
    out, refs = refs[0], refs[1:]
    if which == 0 and plan.joined:
        (left, across, diag), refs = refs[:3], refs[3:]
        above = below = refs[18]
    elif which == 0:
        (left, above, below, diag), refs = refs[:4], refs[4:]
    bits, weights, slots = refs[0], refs[1:4], (refs[4:11], refs[11:18])
    pairs = paired(list(range(len(windows))))
    start = lax.axis_index("sub") * (plan.c * ROWS)
    clear_pads(slots)
    bits[...] = jnp.ones(bits.shape, f32)
    bits[:, :T] = land[...].astype(f32)
    join_weights(0, sources, weights)

    def row(j):
        return bits[pl.ds(start + plan.index(windows[j]), 1), :]

    def listed(j):
        ident = lax.axis_index("lon") * (plan.c * ROWS * lax.axis_size("sub")) + start + plan.index(windows[j])
        return jnp.max(jnp.where(ocean[...] == ident, 1.0, 0.0), axis=1, keepdims=True)

    def put(t, i, value):
        j = pairs[t][i]
        w = windows[j]
        bottom = jnp.broadcast_to(row(j).astype(bf16), (REC - TP, KP))
        ends = [(out, j, 0)]
        if which == 0:
            ends += [(left, k, 0) for k, v in enumerate(plan.to_left) if v == w]
        for to, k, _ in ends:
            to[k, :T, :] = value
            to[k, TP:, :KP] = bottom
        if which == 0:
            halves = [(above, k, 0) for k, v in enumerate(plan.to_above) if v == w]
            skip = len(plan.to_above) if plan.joined else 0
            halves += [(below, skip + k, LOW) for k, v in enumerate(plan.to_below) if v == w]
            if w == plan.to_diag:
                halves.append((diag, 0, LOW if plan.up else 0))
            for to, k, at in halves:
                end = min(at + HALF, T)
                to[k, : end - at, :] = value[at:end]
                to[k, HALF:, :KP] = bottom[: SENT - HALF]

    def load(t, i):
        return tokens[plan.index(windows[pairs[t][i]])].astype(f32)

    blocks(
        pairs, load, load, lambda t: [row(j) for j in pairs[t]], lambda t, i: listed(pairs[t][i]), put, weights, slots
    )
    if which == 0 and plan.joined:
        for k in range(len(plan.to_above)):
            down = above[len(plan.to_above) + min(k, len(plan.to_below) - 1)].astype(f32)
            across[k] = jnp.where(lax.axis_index("lat") == 0, down, above[k].astype(f32)).astype(bf16)


def second_kernel(plan, which, d, *refs):
    firsts = refs[: 2 if plan.first_b else 1]
    refs = refs[len(firsts) :]
    sources, refs = refs[:4], refs[4 + which :]
    if which == 0 and plan.joined:
        (right, above, diag), refs = refs[:3], refs[3:]
        below = above
    elif which == 0:
        (right, above, below, diag), refs = refs[:4], refs[4:]
    out, refs = refs[0], refs[1:]
    if which == 0 and plan.joined:
        (to_right, across, to_diag, edge), refs = refs[:4], refs[4:]
    elif which == 0:
        (to_right, to_below, to_above, to_diag), refs = refs[:4], refs[4:]
    kept, left = refs[:2]
    weights, slots = refs[2:5], (refs[5:12], refs[12:19])
    side_masks(left)
    clear_pads(slots)
    join_weights(1, sources, weights)
    c = plan.c
    windows = plan.rest if which else plan.some
    all_windows = list(windows) if which else windows + plan.lower + plan.upper

    def record(x, r):
        if r == ROWS:
            return (above, x, 0, HALF) if x < len(plan.to_above) else (diag, 0, 0, HALF)
        if r < 0:
            return (below, x - plan.low, LOW, HALF) if x < c else (diag, 0, LOW, HALF)
        if x == c:
            return right, r, 0, TP
        if (x, r) in plan.first_a:
            return firsts[0], plan.first_a.index((x, r)), 0, TP
        return firsts[1], plan.first_b.index((x, r)), 0, TP

    token = lax.broadcasted_iota(jnp.int32, (1, KP), 1)
    left_row, top_row = token % WW < WW // 2, token < T // 2

    def gathered(x, r):
        def at(i, j, rows):
            ref, k, base, _ = record(x + i, r + j)
            return ref[k, rows.start - base : rows.stop - base, :]

        return merged(at, left, d)

    def land_of(x, r):
        a, b, e, f = [
            ref[k, at : at + 16, :KP].astype(f32)[:1]
            for ref, k, _, at in (record(x + i, r + j) for j in (0, 1) for i in (0, 1))
        ]
        return jnp.where(
            token < T, jnp.where(top_row, jnp.where(left_row, f, e), jnp.where(left_row, b, a)), 1.0
        )

    def store(n, value):
        out[n] = value
        if which:
            return
        w = all_windows[n]
        if w in plan.back_right:
            to_right[plan.back_right.index(w)] = value
        if w in plan.lower and not plan.joined:
            to_below[plan.lower.index(w)] = value[:HALF]
        if w in plan.upper and not plan.joined:
            to_above[plan.upper.index(w)] = value[LOW:]
        if w == (plan.back_right[0] if plan.up else plan.back_right[-1]):
            to_diag[0] = value[LOW:] if plan.up else value[:HALF]

    band, bands = lax.axis_index("lat"), lax.axis_size("lat")
    base = len(windows)
    lower_set = band < bands - 1 if plan.up else band >= 0
    on = jnp.where(lower_set, band < bands - 1, band > 0).astype(f32)

    def either(a, b):
        return jnp.where(lower_set, a.astype(f32), b.astype(f32)).astype(a.dtype)

    def window(place):
        if place[0] != "set":
            return gathered(*place)
        j = place[1]
        low = gathered(*plan.lower[j])
        return either(low, gathered(*plan.upper[min(j, len(plan.upper) - 1)])) if plan.up else low

    def land(place):
        if place[0] != "set":
            return land_of(*place)
        j = place[1]
        low = land_of(*plan.lower[j])
        return either(low, land_of(*plan.upper[min(j, len(plan.upper) - 1)])) if plan.up else low

    def finish(place, value):
        if place[0] != "set":
            return store(all_windows.index(place), value)
        j = place[1]
        if not plan.up:
            return store(base + j, value)
        if plan.joined:
            across[j, : T - LOW] = either(value[: T - LOW], value[LOW:])
            across[j, T - LOW :] = value[T - LOW : HALF]
        store(base + j, either(value, gathered(*plan.lower[j])))
        if j < len(plan.upper):
            store(base + len(plan.lower) + j, either(gathered(*plan.upper[j]), value))

    def run(places, keep):
        pairs = paired(places)

        def load(t, i):
            value = window(pairs[t][i])
            kept[2 * (t % 3) + i] = value
            return value.astype(f32)

        def again(t, i):
            return kept[2 * (t % 3) + i].astype(f32)

        blocks(
            pairs, load, again, lambda t: [land(p) for p in pairs[t]], lambda t, i: keep(pairs[t][i]),
            lambda t, i, value: finish(pairs[t][i], value), weights, slots,
        )

    if which == 0 and plan.joined:
        for x in range(c):
            (a, i, _, _), (b, j, _, _) = record(x, 0), record(x, ROWS - 1)
            edge[x] = either(a[i, :HALF, :], b[j, LOW : LOW + HALF, :])

    moving = [] if which else [("set", j) for j in range(len(plan.lower))]
    run(list(windows) + moving, lambda place: on if place[0] == "set" else 1.0)
    if which == 0 and plan.up and bands > 2:

        @pl.when((band > 0) & (band < bands - 1))
        def _():
            run(plan.upper, lambda place: 1.0)


def place_kernel(plan, which, d, *refs):
    (raw_c, raw_d, lefts, aboves), refs = refs[:4], refs[4:]
    (belows, refs) = (aboves, refs) if plan.joined else (refs[0], refs[1:])
    corner, refs = refs[0], refs[1:]
    if plan.joined:
        edge, refs = refs[0], refs[1:]
    out, fin, left, sem_out = refs[which:]
    c = plan.c
    side_masks(left)
    where = {}
    for j, w in enumerate(plan.some + plan.lower + plan.upper):
        where[w] = (raw_c, j, 0)
    for j, w in enumerate(plan.rest):
        where[w] = (raw_d, j, 0)
    for k, (_, r) in enumerate(plan.back_right):
        where[-1, r] = (lefts, k, 0)
    for k, (x, _) in enumerate(plan.lower):
        where[x, -1] = (aboves, k, 0)
    for k, (x, _) in enumerate(plan.upper):
        where[x, ROWS - 1] = (belows, k, LOW)
    where[(-1, ROWS - 1) if plan.up else (-1, -1)] = (corner, 0, LOW if plan.up else 0)
    me = lax.axis_index("sub")
    start = (1 - me if which else me) * (c * ROWS)
    copies = []

    def keep_edge(w, x, first, band):
        low = LOW if first else 0
        rows = slice(low, min(low + HALF, T))
        token = lax.broadcasted_iota(jnp.int32, (rows.stop - low, d), 0) + low
        own = (lax.axis_index("lat") == band) & (token >= first) & (token < first + T // 2)
        value = jnp.where(own, edge[x, : rows.stop - low].astype(f32), fin[w, rows].astype(f32))
        fin[w, rows] = value.astype(bf16)

    for x in range(c):
        for r in range(ROWS):
            w = x * ROWS + r

            def at(i, j, rows, x=x, r=r):
                ref, k, base = where[x - i, r - j]
                return ref[k, rows.start - base : rows.stop - base, :]

            fin[w] = merged(at, left, d)
            if plan.joined and r == 0:
                keep_edge(w, x, 0, 0)
            if plan.joined and r == ROWS - 1:
                keep_edge(w, x, T // 2, 1)
            copies.append(pltpu.make_async_copy(fin.at[w], out.at[start + w], sem_out.at[w]))
            copies[-1].start()
    for copy in copies:
        copy.wait()


def ring(value, axes, by):
    sizes = [lax.axis_size(a) for a in axes]
    total = int(np.prod(sizes))
    grid = np.arange(total).reshape(sizes)
    moved = grid
    for dim, step in enumerate(by):
        moved = np.roll(moved, -step, axis=dim)
    pairs = list(zip(grid.ravel().tolist(), moved.ravel().tolist()))
    return lax.ppermute(value, tuple(axes), pairs)


def beside(value, lat, step):
    lon, sub, lats = lax.axis_size("lon"), lax.axis_size("sub"), lax.axis_size("lat")
    ident = np.arange(lon * lats * sub).reshape(lon, lats, sub)
    line = np.transpose(ident, (1, 0, 2)).reshape(lats, lon * sub)
    axes = ("lon", "lat", "sub")
    if not lat:
        line, axes = np.arange(lon * sub)[None], ("lon", "sub")
    moved = np.roll(line, (-lat, -step), axis=(0, 1))
    return lax.ppermute(value, axes, list(zip(line.ravel().tolist(), moved.ravel().tolist())))


def call(body, ins, outs, scratch, alias, flops, limit, where):
    total = sum(int(np.prod(o.shape)) * 2 for o in outs)
    return pl.pallas_call(
        body, in_specs=ins, out_specs=[where] * len(outs), out_shape=outs, scratch_shapes=scratch,
        input_output_aliases=alias,
        compiler_params=pltpu.CompilerParams(vmem_limit_bytes=limit * 2**20),
        cost_estimate=pl.CostEstimate(flops=flops, bytes_accessed=2 * total, transcendentals=0),
    )


def shards(tokens, land_bits, ocean_list, w_qkv, w_out):
    window_count, _, d = tokens.shape
    mine = window_count // lax.axis_size("sub")
    plan = Plan(mine // ROWS, lax.axis_size("lat"))
    turned = jnp.swapaxes(w_qkv, 2, 3)
    other_qkv, other_out = ring((turned, w_out), ("sub",), (1,))
    per_window = 12_000_000_000

    def shape(*s):
        return jax.ShapeDtypeStruct(s, bf16)

    brought = call(
        functools.partial(bring_kernel, plan), [HBM] + [VMEM] * 4, [shape(mine, T, d)],
        [pltpu.SemaphoreType.DMA], {}, 1_000_000, BRING, VMEM,
    )(tokens, land_bits, ocean_list, turned, w_out)[0]
    weights = (turned, w_out, other_qkv, other_out)
    slot = [
        pltpu.VMEM((2 * TP, d), bf16), pltpu.VMEM((2 * TP, 2 * d), bf16), pltpu.VMEM((2, d, TP), bf16),
        pltpu.VMEM((2, d, TP), bf16), pltpu.VMEM((2 * TP, d), bf16), pltpu.VMEM((2, TP, 128), bf16),
        pltpu.VMEM((KP, 8), f32),
    ]
    work = [pltpu.VMEM((2 * d, d), bf16), pltpu.VMEM((d, d), bf16), pltpu.VMEM((d, d), bf16)] + slot + slot

    def first_call(which, outs):
        n = len(plan.first_b if which else plan.first_a)
        return call(
            functools.partial(first_kernel, plan, which), [VMEM] * 7, outs,
            [pltpu.VMEM((window_count, KP), f32)] + work + [pltpu.VMEM((plan.c + 1, SENT, d), bf16)], {},
            n * per_window, LIMIT, VMEM,
        )(brought, land_bits, ocean_list, *weights)

    counts = (len(plan.to_above), max(len(plan.to_below), 1))
    halves = [shape(n, SENT, d) for n in (counts[:1] if plan.joined else counts) + (1,)]
    first_a, left, *bands, diag = first_call(0, [shape(len(plan.first_a), REC, d), shape(ROWS, REC, d)] + halves)
    right = beside(left, 0, -1)
    bands[0] = ring(bands[0], ("lat",), (-1,))
    if plan.up and not plan.joined:
        bands[1] = ring(bands[1], ("lat",), (1,))
    from_diag = beside(diag, 1 if plan.up else -1, -1)
    firsts = (first_a,)
    if plan.first_b:
        firsts += tuple(first_call(1, [shape(len(plan.first_b), REC, d)]))

    def second_call(which, ins, outs):
        scratch = [pltpu.VMEM((6, T, d), bf16), pltpu.VMEM((T, 128), bf16)] + work
        return call(
            functools.partial(second_kernel, plan, which, d), [VMEM] * len(ins), outs, scratch,
            {}, outs[0].shape[0] * per_window, LIMIT, VMEM,
        )(*ins)

    rim = len(plan.some) + len(plan.lower) + len(plan.upper)
    counts = (len(plan.lower), max(len(plan.upper), 1))
    backs = [shape(counts[0], HALF, d)] if plan.joined else [shape(counts[0], HALF, d), shape(counts[1], T - LOW, d)]
    raw_c, to_right, *backs = second_call(
        0,
        firsts + weights + (right, *bands, from_diag),
        [
            shape(rim, T, d), shape(ROWS, T, d), *backs, shape(1, T - LOW if plan.up else HALF, d),
        ] + ([shape(plan.c, HALF, d)] if plan.joined else []),
    )
    edge = (backs.pop(),) if plan.joined else ()
    to_diag = backs.pop()
    lefts = beside(to_right, 0, 1)
    backs[0] = ring(backs[0], ("lat",), (1,))
    if plan.up and not plan.joined:
        backs[1] = ring(backs[1], ("lat",), (-1,))
    corner = beside(to_diag, -1 if plan.up else 1, 1)
    other_c = ring(raw_c, ("sub",), (1,))
    other_edge = (ring(edge[0], ("sub",), (1,)),) if plan.joined else ()
    raw_d = raw_c
    if plan.rest:
        raw_d = second_call(1, firsts + weights + (to_diag,), [shape(len(plan.rest), T, d)])[0]
    other_d = ring(raw_d, ("sub",), (1,)) if plan.rest else other_c
    here = (lefts, *backs, corner)
    there = ring(here, ("sub",), (1,))

    def place_call(which, *ins):
        return call(
            functools.partial(place_kernel, plan, which, d), [VMEM] * (len(ins) - which) + [HBM] * which,
            [shape(window_count, T, d)],
            [pltpu.VMEM((mine, T, d), bf16), pltpu.VMEM((T, 128), bf16), pltpu.SemaphoreType.DMA((mine,))],
            {len(ins) - 1: 0} if which else {}, 100_000_000, LIMIT, HBM,
        )(*ins)[0]

    out = place_call(0, raw_c, raw_d, *here, *edge)
    return place_call(1, other_c, other_d, *there, *other_edge, out)


def solution(mesh):
    placed = (
        P(("groups", "lat", "lon"), None, None),
        P(("groups", "lat", "lon"), None),
        P(("groups", "lat"), None),
        P(None, None, None, "sub"),
        P(None, "sub", None),
    )
    return jax.shard_map(
        shards,
        mesh=mesh,
        in_specs=placed,
        out_specs=P(("groups", "lat", "lon"), None, None),
        check_vma=False,
    )
```

profile of v0, /device:TPU:0, one launch (start us, length us, event | category | flops | bytes accessed | tf_op | source)
XLA Modules:
  0.0 66.4 jit_solution(15103884817418711620)
XLA Ops:
  0.0 0.5 collective-permute-start
  0.5 1.2 %copy-done = bf16[2,3,384,192]{2,3,1,0:T(8,128)(2,1)S(1)} copy-done((bf16[2,3,384,192]{2,3,1,0:T(8,128)(2,1)S(1)}, bf16[2,3,384,192]{2,3,1,0:T(8,128)(2,1)}, u32[]{:S(2)}) %copy-start) | copy-done | bytes 884760
  1.7 1.0 %copy-done.1 = bf16[2,192,384]{2,1,0:T(8,128)(2,1)S(1)} copy-done((bf16[2,192,384]{2,1,0:T(8,128)(2,1)S(1)}, bf16[2,192,384]{2,1,0:T(8,128)(2,1)}, u32[]{:S(2)}) %copy-start.1) | copy-done | bytes 294936
  2.6 0.8 %copy-done.2 = s32[32,200]{1,0:T(8,128)S(1)} copy-done((s32[32,200]{1,0:T(8,128)S(1)}, s32[32,200]{1,0:T(8,128)}, u32[]{:S(2)}) %copy-start.2) | copy-done | bytes 25624
  3.4 0.7 copy-done.3
  4.1 1.7 %shard_map.55.refs_0_ = bf16[16,200,384]{2,1,0:T(8,128)(2,1)S(1)} custom-call(bf16[32,200,384]{2,1,0:T(8,128)(2,1)} %tokens.1, s32[32,200]{1,0:T(8,128)S(1)} %copy-done.2, s32[1,128]{1,0:T(1,128)S(1)} %copy-done.3, bf16[2,3,192,384]{3,2,1,0:T(8,128)(2,1)S(1)} %bitcast.2, bf16[2,192,384]{2,1,0:T(8,128)(2,1)S(1)} %copy-done.1), custom_call_target="tpu_custom_call" | custom-call | flops 1000000 | bytes 4915200 | tf_op jit(solution)/shard_map/pallas_call | solution.py:508
  5.8 9.1 %shard_map.56 = (bf16[8,224,384]{2,1,0:T(8,128)(2,1)S(1)}, bf16[4,224,384]{2,1,0:T(8,128)(2,1)S(1)}, bf16[3,128,384]{2,1,0:T(8,128)(2,1)S(1)}, bf16[1,128,384]{2,1,0:T(8,128)(2,1)S(1)}) custom-call(bf16[16,200,384]{2,1,0:T(8,128)(2,1)S(1)} %shard_map.55.refs_0_, s32[32,200]{1,0:T(8,128)S(1)} %copy-done.2, s32[1,128]{1,0:T(1,128)S(1)} %copy-done.3, ...), custom_call_target="tpu_custom_call" | custom-call | flops 96000000000 | bytes 4915200 | tf_op jit(solution)/shard_map/pallas_call | solution.py:522
  14.9 5.7 %collective-permute-start.4 = (bf16[1,128,384]{2,1,0:T(8,128)(2,1)S(1)}, bf16[1,128,384]{2,1,0:T(8,128)(2,1)S(1)}, u32[]{:S(2)}, u32[]{:S(2)}) collective-permute-start(bf16[1,128,384]{2,1,0:T(8,128)(2,1)S(1)} %get-tuple-element.17), channel_id=1, source_target_pairs={{0,15},{1,2},{4,3},{5,6},{8,7},{9,10},{12,11},{13,14},{2,13},{3,0}... | collective-permute-start | bytes 294920 | tf_op jit(solution)/shard_map/ppermute | solution.py:484
  20.5 0.5 collective-permute-start.3
  21.1 0.4 collective-permute-start.2
  21.5 9.0 %shard_map.57.refs_1_ = bf16[8,224,384]{2,1,0:T(8,128)(2,1)S(1)} custom-call(bf16[16,200,384]{2,1,0:T(8,128)(2,1)S(1)} %shard_map.55.refs_0_, s32[32,200]{1,0:T(8,128)S(1)} %copy-done.2, s32[1,128]{1,0:T(1,128)S(1)} %copy-done.3, bf16[2,3,192,384]{3,2,1,0:T(8,128)(2,1)S(1)} %bitcast.4, bf16[2,192,384]{2,1,0:T(8,128)(2,1)S(1)} %copy-done.1, ...), custom_call_target="tpu_custom_call" | custom-call | flops 96000000000 | bytes 2752512 | tf_op jit(solution)/shard_map/pallas_call | solution.py:522
  30.5 7.6 %shard_map.58 = (bf16[8,200,384]{2,1,0:T(8,128)(2,1)S(1)}, bf16[4,200,384]{2,1,0:T(8,128)(2,1)S(1)}, bf16[2,112,384]{2,1,0:T(8,128)(2,1)S(1)}, bf16[1,104,384]{2,1,0:T(8,128)(2,1)S(1)}, bf16[4,112,384]{2,1,0:T(8,128)(2,1)S(1)}) custom-call(bf16[8,224,384]{2,1,0:T(8,128)(2,1)S(1)} %get-tuple-element.14.refs_0_, bf16[8,224,384]{2,1,0:T(8,128)(2,1)S(1)} %shard_map.57.refs_1_, ...), custom_call_target="tpu_custom_call" | custom-call | flops 96000000000 | bytes 4878336 | tf_op jit(solution)/shard_map/pallas_call | solution.py:542
  38.1 0.2 collective-permute-start.7
  38.2 0.1 collective-permute-start.5
  38.3 9.0 %shard_map.59.refs_1_ = bf16[8,200,384]{2,1,0:T(8,128)(2,1)S(1)} custom-call(bf16[8,224,384]{2,1,0:T(8,128)(2,1)S(1)} %get-tuple-element.14.refs_0_, bf16[8,224,384]{2,1,0:T(8,128)(2,1)S(1)} %shard_map.57.refs_1_, bf16[2,3,192,384]{3,2,1,0:T(8,128)(2,1)S(1)} %bitcast.6, bf16[2,192,384]{2,1,0:T(8,128)(2,1)S(1)} %copy-done.1, ...), custom_call_target="tpu_custom_call" | custom-call | flops 96000000000 | bytes 2457600 | tf_op jit(solution)/shard_map/pallas_call | solution.py:542
  47.3 0.5 collective-permute-start.6
  47.8 1.7 %collective-permute-done.7.refs_2_ = bf16[4,200,384]{2,1,0:T(8,128)(2,1)S(1)} collective-permute-done((bf16[4,200,384]{2,1,0:T(8,128)(2,1)S(1)}, bf16[4,200,384]{2,1,0:T(8,128)(2,1)S(1)}, u32[]{:S(2)}, u32[]{:S(2)}) %collective-permute-start.7) | collective-permute-done | bytes 614432 | tf_op jit(solution)/shard_map/ppermute | solution.py:484
  49.5 1.6 %collective-permute-start.11 = (bf16[1,104,384]{2,1,0:T(8,128)(2,1)S(1)}, bf16[1,104,384]{2,1,0:T(8,128)(2,1)S(1)}, u32[]{:S(2)}, u32[]{:S(2)}) collective-permute-start(bf16[1,104,384]{2,1,0:T(8,128)(2,1)S(1)} %get-tuple-element.19.refs_6_), channel_id=1, source_target_pairs={{0,3},{1,6},{4,7},{5,10},{8,11},{9,14},{12,15},{13,2},{2,1},{3,4},... | collective-permute-start | bytes 239624 | tf_op jit(solution)/shard_map/ppermute | solution.py:484
  51.1 4.9 %collective-permute-done.11.refs_4_ = bf16[1,104,384]{2,1,0:T(8,128)(2,1)S(1)} collective-permute-done((bf16[1,104,384]{2,1,0:T(8,128)(2,1)S(1)}, bf16[1,104,384]{2,1,0:T(8,128)(2,1)S(1)}, u32[]{:S(2)}, u32[]{:S(2)}) %collective-permute-start.11) | collective-permute-done | bytes 79904 | tf_op jit(solution)/shard_map/ppermute | solution.py:484
  56.0 1.5 %collective-permute-start.9 = (bf16[2,112,384]{2,1,0:T(8,128)(2,1)S(1)}, bf16[2,112,384]{2,1,0:T(8,128)(2,1)S(1)}, u32[]{:S(2)}, u32[]{:S(2)}) collective-permute-start(bf16[2,112,384]{2,1,0:T(8,128)(2,1)S(1)} %get-tuple-element.21), channel_id=1, source_target_pairs={{0,2},{2,0},{1,3},{3,1},{4,6},{6,4},{5,7},{7,5},{8,10},{10,8},{9,1... | collective-permute-start | bytes 516104 | tf_op jit(solution)/shard_map/ppermute | solution.py:473
  57.5 0.2 collective-permute-start.13
  57.8 5.1 %collective-permute-done.9.refs_3_ = bf16[2,112,384]{2,1,0:T(8,128)(2,1)S(1)} collective-permute-done((bf16[2,112,384]{2,1,0:T(8,128)(2,1)S(1)}, bf16[2,112,384]{2,1,0:T(8,128)(2,1)S(1)}, u32[]{:S(2)}, u32[]{:S(2)}) %collective-permute-start.9) | collective-permute-done | bytes 172064 | tf_op jit(solution)/shard_map/ppermute | solution.py:473
  62.8 1.7 %shard_map.60.refs_6_ = bf16[32,200,384]{2,1,0:T(8,128)(2,1)} custom-call(bf16[8,200,384]{2,1,0:T(8,128)(2,1)S(1)} %get-tuple-element.18.refs_0_, bf16[8,200,384]{2,1,0:T(8,128)(2,1)S(1)} %shard_map.59.refs_1_, bf16[4,200,384]{2,1,0:T(8,128)(2,1)S(1)} %collective-permute-done.7.refs_2_, bf16[2,112,384]{2,1,0:T(8,128)(2,1)S(1)} %collective-permute-done.9.refs_3_, ...), custom_call_target="tpu_custom_call" | custom-call | flops 100000000 | bytes 9830400 | tf_op jit(solution)/shard_map/pallas_call | solution.py:574
  64.6 1.7 %shard_map.61 = bf16[32,200,384]{2,1,0:T(8,128)(2,1)} custom-call(bf16[8,200,384]{2,1,0:T(8,128)(2,1)S(1)} %collective-permute-done.5.refs_0_, bf16[8,200,384]{2,1,0:T(8,128)(2,1)S(1)} %collective-permute-done.6.refs_1_, bf16[4,200,384]{2,1,0:T(8,128)(2,1)S(1)} %collective-permute-done.8.refs_2_, ...), custom_call_target="tpu_custom_call", output_to_operand_aliasing={{}: (6, {})} | custom-call | flops 100000000 | bytes 9830400 | tf_op jit(solution)/shard_map/pallas_call | solution.py:574
  (19 shorter events, 0.1 us)
Async XLA Ops:
  0.0 5.8 %collective-permute-start = (bf16[2,3,192,384]{3,2,1,0:T(8,128)(2,1)}, bf16[2,3,192,384]{3,2,1,0:T(8,128)(2,1)S(1)}, u32[]{:S(2)}, u32[]{:S(2)}) collective-permute-start(bf16[2,3,192,384]{3,2,1,0:T(8,128)(2,1)} %bitcast.1), channel_id=1, source_target_pairs={{0,1},{1,0},{2,3},{3,2},{4,5},{5,4},{6,7},{7,6},{8,9},{9,8},{10,11... | collective-permute-start | bytes 2654216 | tf_op jit(solution)/shard_map/ppermute | solution.py:473
  0.5 5.3 %collective-permute-start.1 = (bf16[2,192,384]{2,1,0:T(8,128)(2,1)}, bf16[2,192,384]{2,1,0:T(8,128)(2,1)S(1)}, u32[]{:S(2)}, u32[]{:S(2)}) collective-permute-start(bf16[2,192,384]{2,1,0:T(8,128)(2,1)} %refs_3_.3), channel_id=1, source_target_pairs={{0,1},{1,0},{2,3},{3,2},{4,5},{5,4},{6,7},{7,6},{8,9},{9,8},{10,11... | collective-permute-start | bytes 884744 | tf_op jit(solution)/shard_map/ppermute | solution.py:473
  0.5 1.2 %copy-start = (bf16[2,3,384,192]{2,3,1,0:T(8,128)(2,1)S(1)}, bf16[2,3,384,192]{2,3,1,0:T(8,128)(2,1)}, u32[]{:S(2)}) copy-start(bf16[2,3,384,192]{2,3,1,0:T(8,128)(2,1)} %param.8) | copy-start | bytes 2654212
  1.7 1.0 %copy-start.1 = (bf16[2,192,384]{2,1,0:T(8,128)(2,1)S(1)}, bf16[2,192,384]{2,1,0:T(8,128)(2,1)}, u32[]{:S(2)}) copy-start(bf16[2,192,384]{2,1,0:T(8,128)(2,1)} %refs_3_.3) | copy-start | bytes 884740
  2.6 0.8 %copy-start.2 = (s32[32,200]{1,0:T(8,128)S(1)}, s32[32,200]{1,0:T(8,128)}, u32[]{:S(2)}) copy-start(s32[32,200]{1,0:T(8,128)} %refs_1_.3) | copy-start | bytes 76804
  3.4 0.7 copy-start.3
  14.9 15.6 %collective-permute-start.4 = (bf16[1,128,384]{2,1,0:T(8,128)(2,1)S(1)}, bf16[1,128,384]{2,1,0:T(8,128)(2,1)S(1)}, u32[]{:S(2)}, u32[]{:S(2)}) collective-permute-start(bf16[1,128,384]{2,1,0:T(8,128)(2,1)S(1)} %get-tuple-element.17), channel_id=1, source_target_pairs={{0,15},{1,2},{4,3},{5,6},{8,7},{9,10},{12,11},{13,14},{2,13},{3,0}... | collective-permute-start | bytes 294920 | tf_op jit(solution)/shard_map/ppermute | solution.py:484
  20.5 10.0 %collective-permute-start.3 = (bf16[3,128,384]{2,1,0:T(8,128)(2,1)S(1)}, bf16[3,128,384]{2,1,0:T(8,128)(2,1)S(1)}, u32[]{:S(2)}, u32[]{:S(2)}) collective-permute-start(bf16[3,128,384]{2,1,0:T(8,128)(2,1)S(1)} %get-tuple-element.16), channel_id=1, source_target_pairs={{0,2},{2,0},{1,3},{3,1},{4,6},{6,4},{5,7},{7,5},{8,10},{10,8},{9,1... | collective-permute-start | bytes 884744 | tf_op jit(solution)/shard_map/ppermute | solution.py:473
  21.1 9.4 %collective-permute-start.2 = (bf16[4,224,384]{2,1,0:T(8,128)(2,1)S(1)}, bf16[4,224,384]{2,1,0:T(8,128)(2,1)S(1)}, u32[]{:S(2)}, u32[]{:S(2)}) collective-permute-start(bf16[4,224,384]{2,1,0:T(8,128)(2,1)S(1)} %get-tuple-element.15), channel_id=1, source_target_pairs={{0,13},{1,0},{4,1},{5,4},{8,5},{9,8},{12,9},{13,12},{2,15},{3,2},{... | collective-permute-start | bytes 2064392 | tf_op jit(solution)/shard_map/ppermute | solution.py:484
  38.1 11.4 %collective-permute-start.7 = (bf16[4,200,384]{2,1,0:T(8,128)(2,1)S(1)}, bf16[4,200,384]{2,1,0:T(8,128)(2,1)S(1)}, u32[]{:S(2)}, u32[]{:S(2)}) collective-permute-start(bf16[4,200,384]{2,1,0:T(8,128)(2,1)S(1)} %get-tuple-element.20), channel_id=1, source_target_pairs={{0,1},{1,4},{4,5},{5,8},{8,9},{9,12},{12,13},{13,0},{2,3},{3,6},{6... | collective-permute-start | bytes 1843208 | tf_op jit(solution)/shard_map/ppermute | solution.py:484
  38.2 26.3 %collective-permute-start.5 = (bf16[8,200,384]{2,1,0:T(8,128)(2,1)S(1)}, bf16[8,200,384]{2,1,0:T(8,128)(2,1)S(1)}, u32[]{:S(2)}, u32[]{:S(2)}) collective-permute-start(bf16[8,200,384]{2,1,0:T(8,128)(2,1)S(1)} %get-tuple-element.18.refs_0_), channel_id=1, source_target_pairs={{0,1},{1,0},{2,3},{3,2},{4,5},{5,4},{6,7},{7,6},{8,9},{9,8},{10,11... | collective-permute-start | bytes 3686408 | tf_op jit(solution)/shard_map/ppermute | solution.py:473
  47.3 17.3 %collective-permute-start.6 = (bf16[8,200,384]{2,1,0:T(8,128)(2,1)S(1)}, bf16[8,200,384]{2,1,0:T(8,128)(2,1)S(1)}, u32[]{:S(2)}, u32[]{:S(2)}) collective-permute-start(bf16[8,200,384]{2,1,0:T(8,128)(2,1)S(1)} %shard_map.59.refs_1_), channel_id=1, source_target_pairs={{0,1},{1,0},{2,3},{3,2},{4,5},{5,4},{6,7},{7,6},{8,9},{9,8},{10,11... | collective-permute-start | bytes 3686408 | tf_op jit(solution)/shard_map/ppermute | solution.py:473
  49.5 15.0 %collective-permute-start.8 = (bf16[4,200,384]{2,1,0:T(8,128)(2,1)S(1)}, bf16[4,200,384]{2,1,0:T(8,128)(2,1)S(1)}, u32[]{:S(2)}, u32[]{:S(2)}) collective-permute-start(bf16[4,200,384]{2,1,0:T(8,128)(2,1)S(1)} %collective-permute-done.7.refs_2_), channel_id=1, source_target_pairs={{0,1},{1,0},{2,3},{3,2},{4,5},{5,4},{6,7},{7,6},{8,9},{9,8},{10,11... | collective-permute-start | bytes 1843208 | tf_op jit(solution)/shard_map/ppermute | solution.py:473
  49.5 6.5 %collective-permute-start.11 = (bf16[1,104,384]{2,1,0:T(8,128)(2,1)S(1)}, bf16[1,104,384]{2,1,0:T(8,128)(2,1)S(1)}, u32[]{:S(2)}, u32[]{:S(2)}) collective-permute-start(bf16[1,104,384]{2,1,0:T(8,128)(2,1)S(1)} %get-tuple-element.19.refs_6_), channel_id=1, source_target_pairs={{0,3},{1,6},{4,7},{5,10},{8,11},{9,14},{12,15},{13,2},{2,1},{3,4},... | collective-permute-start | bytes 239624 | tf_op jit(solution)/shard_map/ppermute | solution.py:484
  56.0 1.5 %collective-permute-start.12 = (bf16[1,104,384]{2,1,0:T(8,128)(2,1)S(1)}, bf16[1,104,384]{2,1,0:T(8,128)(2,1)S(1)}, u32[]{:S(2)}, u32[]{:S(2)}) collective-permute-start(bf16[1,104,384]{2,1,0:T(8,128)(2,1)S(1)} %collective-permute-done.11.refs_4_), channel_id=1, source_target_pairs={{0,1},{1,0},{2,3},{3,2},{4,5},{5,4},{6,7},{7,6},{8,9},{9,8},{10,11... | collective-permute-start | bytes 239624 | tf_op jit(solution)/shard_map/ppermute | solution.py:473
  56.0 6.8 %collective-permute-start.9 = (bf16[2,112,384]{2,1,0:T(8,128)(2,1)S(1)}, bf16[2,112,384]{2,1,0:T(8,128)(2,1)S(1)}, u32[]{:S(2)}, u32[]{:S(2)}) collective-permute-start(bf16[2,112,384]{2,1,0:T(8,128)(2,1)S(1)} %get-tuple-element.21), channel_id=1, source_target_pairs={{0,2},{2,0},{1,3},{3,1},{4,6},{6,4},{5,7},{7,5},{8,10},{10,8},{9,1... | collective-permute-start | bytes 516104 | tf_op jit(solution)/shard_map/ppermute | solution.py:473
  57.5 7.0 %collective-permute-start.13 = (bf16[4,112,384]{2,1,0:T(8,128)(2,1)S(1)}, bf16[4,112,384]{2,1,0:T(8,128)(2,1)S(1)}, u32[]{:S(2)}, u32[]{:S(2)}) collective-permute-start(bf16[4,112,384]{2,1,0:T(8,128)(2,1)S(1)} %get-tuple-element.22.refs_5_), channel_id=1, source_target_pairs={{0,1},{1,0},{2,3},{3,2},{4,5},{5,4},{6,7},{7,6},{8,9},{9,8},{10,11... | collective-permute-start | bytes 1032200 | tf_op jit(solution)/shard_map/ppermute | solution.py:473
  62.8 1.7 %collective-permute-start.10 = (bf16[2,112,384]{2,1,0:T(8,128)(2,1)S(1)}, bf16[2,112,384]{2,1,0:T(8,128)(2,1)S(1)}, u32[]{:S(2)}, u32[]{:S(2)}) collective-permute-start(bf16[2,112,384]{2,1,0:T(8,128)(2,1)S(1)} %collective-permute-done.9.refs_3_), channel_id=1, source_target_pairs={{0,1},{1,0},{2,3},{3,2},{4,5},{5,4},{6,7},{7,6},{8,9},{9,8},{10,11... | collective-permute-start | bytes 516104 | tf_op jit(solution)/shard_map/ppermute | solution.py:473
where the time goes:
time: 66.7 us; the launch traced here: 66.4 us
  Pallas kernels  39.7 us (60%)
  waiting for transfers between devices  11.7 us (18%)
  starting transfers between devices  11.2 us (17%)
  local copies, waits for them, and re-layouts  3.54 us (5%)
    pallas_call x2, Pallas kernels, first_call(): call(functools.partial(first_kernel, plan, which), [VMEM] * 7, outs, [plt...  18.1 us
    pallas_call x2, Pallas kernels, second_call(): call(functools.partial(second_kernel, plan, which, d), [VMEM] * len(ins),...  16.5 us
    ppermute x4, starting transfers between devices, beside(): lax.ppermute(value, axes, list(zip(line.ravel().tolist(), moved.ravel().t...  7.84 us
    ppermute x4, waiting for transfers between devices, beside(): lax.ppermute(value, axes, list(zip(line.ravel().tolist(), moved.ravel().t...  6.65 us
    ppermute x10, waiting for transfers between devices, ring(): return lax.ppermute(value, tuple(axes), pairs)  5.09 us
    unnamed x8, local copies, waits for them, and re-layouts  3.54 us
    pallas_call x2, Pallas kernels, place_call(): call(functools.partial(place_kernel, plan, which, d), [VMEM] * (len(ins)...  3.35 us
    ppermute x10, starting transfers between devices, ring(): return lax.ppermute(value, tuple(axes), pairs)  3.32 us
  transfers between devices with their start and end apart: 14, of which 3 were waited for; matrix products, arithmetic and copies ran while one was open for 0% of the time, Pallas kernels for 32%

commit v1 on v0

--- a/solution.py
+++ b/solution.py
@@ -213,7 +213,7 @@
         return window[0] * ROWS + window[1]
 
 
-def bring_kernel(plan, tokens, land, ocean, qkv, out, mine, sem):
+def bring_kernel(plan, tokens, qkv, mine, sem):
     start = lax.axis_index("sub") * (plan.c * ROWS)
     copy = pltpu.make_async_copy(tokens.at[pl.ds(start, plan.c * ROWS)], mine, sem)
     copy.start()
@@ -506,9 +506,9 @@
         return jax.ShapeDtypeStruct(s, bf16)
 
     brought = call(
-        functools.partial(bring_kernel, plan), [HBM] + [VMEM] * 4, [shape(mine, T, d)],
+        functools.partial(bring_kernel, plan), [HBM, VMEM], [shape(mine, T, d)],
         [pltpu.SemaphoreType.DMA], {}, 1_000_000, BRING, VMEM,
-    )(tokens, land_bits, ocean_list, turned, w_out)[0]
+    )(tokens, turned)[0]
     weights = (turned, w_out, other_qkv, other_out)
     slot = [
         pltpu.VMEM((2 * TP, d), bf16), pltpu.VMEM((2 * TP, 2 * d), bf16), pltpu.VMEM((2, d, TP), bf16),

time: 66.7 us -> 64.1 us (0.961)
  local copies, waits for them, and re-layouts: 3.54 us -> 1.18 us
    unnamed x8, local copies, waits for them, and re-layouts: 3.54 us -> 1.18 us
  transfers between devices with their start and end apart: 14 -> 14, of which waited for: 3 -> 3; matrix products, arithmetic and copies ran while one was open for 0% -> 0% of each run, Pallas kernels for 32% -> 33%
where the time goes in v1:
time: 64.1 us; the launch traced here: 64 us
  Pallas kernels  39.5 us (62%)
  waiting for transfers between devices  11.7 us (18%)
  starting transfers between devices  11.3 us (18%)
  local copies, waits for them, and re-layouts  1.18 us (2%)
    pallas_call x2, Pallas kernels, first_call(): call(functools.partial(first_kernel, plan, which), [VMEM] * 7, outs, [plt...  18 us
    pallas_call x2, Pallas kernels, second_call(): call(functools.partial(second_kernel, plan, which, d), [VMEM] * len(ins),...  16.5 us
    ppermute x4, starting transfers between devices, beside(): lax.ppermute(value, axes, list(zip(line.ravel().tolist(), moved.ravel().t...  7.86 us
    ppermute x4, waiting for transfers between devices, beside(): lax.ppermute(value, axes, list(zip(line.ravel().tolist(), moved.ravel().t...  6.59 us
    ppermute x10, waiting for transfers between devices, ring(): return lax.ppermute(value, tuple(axes), pairs)  5.06 us
    ppermute x10, starting transfers between devices, ring(): return lax.ppermute(value, tuple(axes), pairs)  3.41 us
    pallas_call x2, Pallas kernels, place_call(): call(functools.partial(place_kernel, plan, which, d), [VMEM] * (len(ins)...  3.35 us
    pallas_call x1, Pallas kernels, shards(): call(functools.partial(bring_kernel, plan), [HBM, VMEM], [shape(mine, T,...  1.75 us
  transfers between devices with their start and end apart: 14, of which 3 were waited for; matrix products, arithmetic and copies ran while one was open for 0% of the time, Pallas kernels for 33%

profile of v1, /device:TPU:0, one launch (start us, length us, event | category | flops | bytes accessed | tf_op | source)
XLA Modules:
  0.0 64.0 jit_solution(17233893620365788084)
XLA Ops:
  0.0 0.5 collective-permute-start
  0.5 0.1 collective-permute-start.1
  0.6 1.2 %copy-done = bf16[2,3,384,192]{2,3,1,0:T(8,128)(2,1)S(1)} copy-done((bf16[2,3,384,192]{2,3,1,0:T(8,128)(2,1)S(1)}, bf16[2,3,384,192]{2,3,1,0:T(8,128)(2,1)}, u32[]{:S(2)}) %copy-start) | copy-done | bytes 884760
  1.7 1.7 %shard_map.55.refs_0_ = bf16[16,200,384]{2,1,0:T(8,128)(2,1)S(1)} custom-call(bf16[32,200,384]{2,1,0:T(8,128)(2,1)} %tokens.1, bf16[2,3,192,384]{3,2,1,0:T(8,128)(2,1)S(1)} %bitcast.2), custom_call_target="tpu_custom_call" | custom-call | flops 1000000 | bytes 4915200 | tf_op jit(solution)/shard_map/pallas_call | solution.py:508
  3.5 0.0 collective-permute-done.1.refs_6_.refs_5_
  3.5 9.0 %shard_map.56 = (bf16[8,224,384]{2,1,0:T(8,128)(2,1)S(1)}, bf16[4,224,384]{2,1,0:T(8,128)(2,1)S(1)}, bf16[3,128,384]{2,1,0:T(8,128)(2,1)S(1)}, bf16[1,128,384]{2,1,0:T(8,128)(2,1)S(1)}) custom-call(bf16[16,200,384]{2,1,0:T(8,128)(2,1)S(1)} %shard_map.55.refs_0_, s32[32,200]{1,0:T(8,128)S(1)} %copy-done.2, s32[1,128]{1,0:T(1,128)S(1)} %copy-done.3, ...), custom_call_target="tpu_custom_call" | custom-call | flops 96000000000 | bytes 4915200 | tf_op jit(solution)/shard_map/pallas_call | solution.py:522
  12.6 5.7 %collective-permute-start.4 = (bf16[1,128,384]{2,1,0:T(8,128)(2,1)S(1)}, bf16[1,128,384]{2,1,0:T(8,128)(2,1)S(1)}, u32[]{:S(2)}, u32[]{:S(2)}) collective-permute-start(bf16[1,128,384]{2,1,0:T(8,128)(2,1)S(1)} %get-tuple-element.17), channel_id=1, source_target_pairs={{0,15},{1,2},{4,3},{5,6},{8,7},{9,10},{12,11},{13,14},{2,13},{3,0}... | collective-permute-start | bytes 294920 | tf_op jit(solution)/shard_map/ppermute | solution.py:484
  18.2 0.5 collective-permute-start.3
  18.8 0.3 collective-permute-start.2
  19.1 8.9 %shard_map.57.refs_1_ = bf16[8,224,384]{2,1,0:T(8,128)(2,1)S(1)} custom-call(bf16[16,200,384]{2,1,0:T(8,128)(2,1)S(1)} %shard_map.55.refs_0_, s32[32,200]{1,0:T(8,128)S(1)} %copy-done.2, s32[1,128]{1,0:T(1,128)S(1)} %copy-done.3, bf16[2,3,192,384]{3,2,1,0:T(8,128)(2,1)S(1)} %bitcast.4, bf16[2,192,384]{2,1,0:T(8,128)(2,1)S(1)} %copy-done.1, ...), custom_call_target="tpu_custom_call" | custom-call | flops 96000000000 | bytes 2752512 | tf_op jit(solution)/shard_map/pallas_call | solution.py:522
  28.0 0.0 collective-permute-done.4.refs_8_
  28.1 7.5 %shard_map.58 = (bf16[8,200,384]{2,1,0:T(8,128)(2,1)S(1)}, bf16[4,200,384]{2,1,0:T(8,128)(2,1)S(1)}, bf16[2,112,384]{2,1,0:T(8,128)(2,1)S(1)}, bf16[1,104,384]{2,1,0:T(8,128)(2,1)S(1)}, bf16[4,112,384]{2,1,0:T(8,128)(2,1)S(1)}) custom-call(bf16[8,224,384]{2,1,0:T(8,128)(2,1)S(1)} %get-tuple-element.14.refs_0_, bf16[8,224,384]{2,1,0:T(8,128)(2,1)S(1)} %shard_map.57.refs_1_, ...), custom_call_target="tpu_custom_call" | custom-call | flops 96000000000 | bytes 4878336 | tf_op jit(solution)/shard_map/pallas_call | solution.py:542
  35.6 0.2 collective-permute-start.7
  35.8 0.1 collective-permute-start.5
  35.9 8.9 %shard_map.59.refs_1_ = bf16[8,200,384]{2,1,0:T(8,128)(2,1)S(1)} custom-call(bf16[8,224,384]{2,1,0:T(8,128)(2,1)S(1)} %get-tuple-element.14.refs_0_, bf16[8,224,384]{2,1,0:T(8,128)(2,1)S(1)} %shard_map.57.refs_1_, bf16[2,3,192,384]{3,2,1,0:T(8,128)(2,1)S(1)} %bitcast.6, bf16[2,192,384]{2,1,0:T(8,128)(2,1)S(1)} %copy-done.1, ...), custom_call_target="tpu_custom_call" | custom-call | flops 96000000000 | bytes 2457600 | tf_op jit(solution)/shard_map/pallas_call | solution.py:542
  44.9 0.5 collective-permute-start.6
  45.4 1.7 %collective-permute-done.7.refs_2_ = bf16[4,200,384]{2,1,0:T(8,128)(2,1)S(1)} collective-permute-done((bf16[4,200,384]{2,1,0:T(8,128)(2,1)S(1)}, bf16[4,200,384]{2,1,0:T(8,128)(2,1)S(1)}, u32[]{:S(2)}, u32[]{:S(2)}) %collective-permute-start.7) | collective-permute-done | bytes 614432 | tf_op jit(solution)/shard_map/ppermute | solution.py:484
  47.0 1.6 %collective-permute-start.11 = (bf16[1,104,384]{2,1,0:T(8,128)(2,1)S(1)}, bf16[1,104,384]{2,1,0:T(8,128)(2,1)S(1)}, u32[]{:S(2)}, u32[]{:S(2)}) collective-permute-start(bf16[1,104,384]{2,1,0:T(8,128)(2,1)S(1)} %get-tuple-element.19.refs_6_), channel_id=1, source_target_pairs={{0,3},{1,6},{4,7},{5,10},{8,11},{9,14},{12,15},{13,2},{2,1},{3,4},... | collective-permute-start | bytes 239624 | tf_op jit(solution)/shard_map/ppermute | solution.py:484
  48.7 4.9 %collective-permute-done.11.refs_4_ = bf16[1,104,384]{2,1,0:T(8,128)(2,1)S(1)} collective-permute-done((bf16[1,104,384]{2,1,0:T(8,128)(2,1)S(1)}, bf16[1,104,384]{2,1,0:T(8,128)(2,1)S(1)}, u32[]{:S(2)}, u32[]{:S(2)}) %collective-permute-start.11) | collective-permute-done | bytes 79904 | tf_op jit(solution)/shard_map/ppermute | solution.py:484
  53.6 1.5 %collective-permute-start.9 = (bf16[2,112,384]{2,1,0:T(8,128)(2,1)S(1)}, bf16[2,112,384]{2,1,0:T(8,128)(2,1)S(1)}, u32[]{:S(2)}, u32[]{:S(2)}) collective-permute-start(bf16[2,112,384]{2,1,0:T(8,128)(2,1)S(1)} %get-tuple-element.21), channel_id=1, source_target_pairs={{0,2},{2,0},{1,3},{3,1},{4,6},{6,4},{5,7},{7,5},{8,10},{10,8},{9,1... | collective-permute-start | bytes 516104 | tf_op jit(solution)/shard_map/ppermute | solution.py:473
  55.1 0.2 collective-permute-start.13
  55.3 5.0 %collective-permute-done.9.refs_3_ = bf16[2,112,384]{2,1,0:T(8,128)(2,1)S(1)} collective-permute-done((bf16[2,112,384]{2,1,0:T(8,128)(2,1)S(1)}, bf16[2,112,384]{2,1,0:T(8,128)(2,1)S(1)}, u32[]{:S(2)}, u32[]{:S(2)}) %collective-permute-start.9) | collective-permute-done | bytes 172064 | tf_op jit(solution)/shard_map/ppermute | solution.py:473
  60.4 1.7 %shard_map.60.refs_6_ = bf16[32,200,384]{2,1,0:T(8,128)(2,1)} custom-call(bf16[8,200,384]{2,1,0:T(8,128)(2,1)S(1)} %get-tuple-element.18.refs_0_, bf16[8,200,384]{2,1,0:T(8,128)(2,1)S(1)} %shard_map.59.refs_1_, bf16[4,200,384]{2,1,0:T(8,128)(2,1)S(1)} %collective-permute-done.7.refs_2_, bf16[2,112,384]{2,1,0:T(8,128)(2,1)S(1)} %collective-permute-done.9.refs_3_, ...), custom_call_target="tpu_custom_call" | custom-call | flops 100000000 | bytes 9830400 | tf_op jit(solution)/shard_map/pallas_call | solution.py:574
  62.1 1.7 %shard_map.61 = bf16[32,200,384]{2,1,0:T(8,128)(2,1)} custom-call(bf16[8,200,384]{2,1,0:T(8,128)(2,1)S(1)} %collective-permute-done.5.refs_0_, bf16[8,200,384]{2,1,0:T(8,128)(2,1)S(1)} %collective-permute-done.6.refs_1_, bf16[4,200,384]{2,1,0:T(8,128)(2,1)S(1)} %collective-permute-done.8.refs_2_, ...), custom_call_target="tpu_custom_call", output_to_operand_aliasing={{}: (6, {})} | custom-call | flops 100000000 | bytes 9830400 | tf_op jit(solution)/shard_map/pallas_call | solution.py:574
  (19 shorter events, 0.0 us)
Async XLA Ops:
  0.0 3.5 %copy-start.3 = (s32[1,128]{1,0:T(1,128)S(1)}, s32[1,128]{1,0:T(1,128)}, u32[]{:S(2)}) copy-start(s32[1,128]{1,0:T(1,128)} %refs_2_.3) | copy-start | bytes 1540
  0.0 3.5 %collective-permute-start = (bf16[2,3,192,384]{3,2,1,0:T(8,128)(2,1)}, bf16[2,3,192,384]{3,2,1,0:T(8,128)(2,1)S(1)}, u32[]{:S(2)}, u32[]{:S(2)}) collective-permute-start(bf16[2,3,192,384]{3,2,1,0:T(8,128)(2,1)} %bitcast.1), channel_id=1, source_target_pairs={{0,1},{1,0},{2,3},{3,2},{4,5},{5,4},{6,7},{7,6},{8,9},{9,8},{10,11... | collective-permute-start | bytes 2654216 | tf_op jit(solution)/shard_map/ppermute | solution.py:473
  0.5 3.0 %collective-permute-start.1 = (bf16[2,192,384]{2,1,0:T(8,128)(2,1)}, bf16[2,192,384]{2,1,0:T(8,128)(2,1)S(1)}, u32[]{:S(2)}, u32[]{:S(2)}) collective-permute-start(bf16[2,192,384]{2,1,0:T(8,128)(2,1)} %refs_3_.3), channel_id=1, source_target_pairs={{0,1},{1,0},{2,3},{3,2},{4,5},{5,4},{6,7},{7,6},{8,9},{9,8},{10,11... | collective-permute-start | bytes 884744 | tf_op jit(solution)/shard_map/ppermute | solution.py:473
  0.6 1.2 %copy-start = (bf16[2,3,384,192]{2,3,1,0:T(8,128)(2,1)S(1)}, bf16[2,3,384,192]{2,3,1,0:T(8,128)(2,1)}, u32[]{:S(2)}) copy-start(bf16[2,3,384,192]{2,3,1,0:T(8,128)(2,1)} %param.8) | copy-start | bytes 2654212
  1.7 1.8 %copy-start.1 = (bf16[2,192,384]{2,1,0:T(8,128)(2,1)S(1)}, bf16[2,192,384]{2,1,0:T(8,128)(2,1)}, u32[]{:S(2)}) copy-start(bf16[2,192,384]{2,1,0:T(8,128)(2,1)} %refs_3_.3) | copy-start | bytes 884740
  1.7 1.8 %copy-start.2 = (s32[32,200]{1,0:T(8,128)S(1)}, s32[32,200]{1,0:T(8,128)}, u32[]{:S(2)}) copy-start(s32[32,200]{1,0:T(8,128)} %refs_1_.3) | copy-start | bytes 76804
  12.6 15.5 %collective-permute-start.4 = (bf16[1,128,384]{2,1,0:T(8,128)(2,1)S(1)}, bf16[1,128,384]{2,1,0:T(8,128)(2,1)S(1)}, u32[]{:S(2)}, u32[]{:S(2)}) collective-permute-start(bf16[1,128,384]{2,1,0:T(8,128)(2,1)S(1)} %get-tuple-element.17), channel_id=1, source_target_pairs={{0,15},{1,2},{4,3},{5,6},{8,7},{9,10},{12,11},{13,14},{2,13},{3,0}... | collective-permute-start | bytes 294920 | tf_op jit(solution)/shard_map/ppermute | solution.py:484
  18.2 9.8 %collective-permute-start.3 = (bf16[3,128,384]{2,1,0:T(8,128)(2,1)S(1)}, bf16[3,128,384]{2,1,0:T(8,128)(2,1)S(1)}, u32[]{:S(2)}, u32[]{:S(2)}) collective-permute-start(bf16[3,128,384]{2,1,0:T(8,128)(2,1)S(1)} %get-tuple-element.16), channel_id=1, source_target_pairs={{0,2},{2,0},{1,3},{3,1},{4,6},{6,4},{5,7},{7,5},{8,10},{10,8},{9,1... | collective-permute-start | bytes 884744 | tf_op jit(solution)/shard_map/ppermute | solution.py:473
  18.8 9.3 %collective-permute-start.2 = (bf16[4,224,384]{2,1,0:T(8,128)(2,1)S(1)}, bf16[4,224,384]{2,1,0:T(8,128)(2,1)S(1)}, u32[]{:S(2)}, u32[]{:S(2)}) collective-permute-start(bf16[4,224,384]{2,1,0:T(8,128)(2,1)S(1)} %get-tuple-element.15), channel_id=1, source_target_pairs={{0,13},{1,0},{4,1},{5,4},{8,5},{9,8},{12,9},{13,12},{2,15},{3,2},{... | collective-permute-start | bytes 2064392 | tf_op jit(solution)/shard_map/ppermute | solution.py:484
  35.6 11.4 %collective-permute-start.7 = (bf16[4,200,384]{2,1,0:T(8,128)(2,1)S(1)}, bf16[4,200,384]{2,1,0:T(8,128)(2,1)S(1)}, u32[]{:S(2)}, u32[]{:S(2)}) collective-permute-start(bf16[4,200,384]{2,1,0:T(8,128)(2,1)S(1)} %get-tuple-element.20), channel_id=1, source_target_pairs={{0,1},{1,4},{4,5},{5,8},{8,9},{9,12},{12,13},{13,0},{2,3},{3,6},{6... | collective-permute-start | bytes 1843208 | tf_op jit(solution)/shard_map/ppermute | solution.py:484
  35.8 26.2 %collective-permute-start.5 = (bf16[8,200,384]{2,1,0:T(8,128)(2,1)S(1)}, bf16[8,200,384]{2,1,0:T(8,128)(2,1)S(1)}, u32[]{:S(2)}, u32[]{:S(2)}) collective-permute-start(bf16[8,200,384]{2,1,0:T(8,128)(2,1)S(1)} %get-tuple-element.18.refs_0_), channel_id=1, source_target_pairs={{0,1},{1,0},{2,3},{3,2},{4,5},{5,4},{6,7},{7,6},{8,9},{9,8},{10,11... | collective-permute-start | bytes 3686408 | tf_op jit(solution)/shard_map/ppermute | solution.py:473
  44.9 17.2 %collective-permute-start.6 = (bf16[8,200,384]{2,1,0:T(8,128)(2,1)S(1)}, bf16[8,200,384]{2,1,0:T(8,128)(2,1)S(1)}, u32[]{:S(2)}, u32[]{:S(2)}) collective-permute-start(bf16[8,200,384]{2,1,0:T(8,128)(2,1)S(1)} %shard_map.59.refs_1_), channel_id=1, source_target_pairs={{0,1},{1,0},{2,3},{3,2},{4,5},{5,4},{6,7},{7,6},{8,9},{9,8},{10,11... | collective-permute-start | bytes 3686408 | tf_op jit(solution)/shard_map/ppermute | solution.py:473
  47.0 15.0 %collective-permute-start.8 = (bf16[4,200,384]{2,1,0:T(8,128)(2,1)S(1)}, bf16[4,200,384]{2,1,0:T(8,128)(2,1)S(1)}, u32[]{:S(2)}, u32[]{:S(2)}) collective-permute-start(bf16[4,200,384]{2,1,0:T(8,128)(2,1)S(1)} %collective-permute-done.7.refs_2_), channel_id=1, source_target_pairs={{0,1},{1,0},{2,3},{3,2},{4,5},{5,4},{6,7},{7,6},{8,9},{9,8},{10,11... | collective-permute-start | bytes 1843208 | tf_op jit(solution)/shard_map/ppermute | solution.py:473
  47.0 6.5 %collective-permute-start.11 = (bf16[1,104,384]{2,1,0:T(8,128)(2,1)S(1)}, bf16[1,104,384]{2,1,0:T(8,128)(2,1)S(1)}, u32[]{:S(2)}, u32[]{:S(2)}) collective-permute-start(bf16[1,104,384]{2,1,0:T(8,128)(2,1)S(1)} %get-tuple-element.19.refs_6_), channel_id=1, source_target_pairs={{0,3},{1,6},{4,7},{5,10},{8,11},{9,14},{12,15},{13,2},{2,1},{3,4},... | collective-permute-start | bytes 239624 | tf_op jit(solution)/shard_map/ppermute | solution.py:484
  53.6 1.5 %collective-permute-start.12 = (bf16[1,104,384]{2,1,0:T(8,128)(2,1)S(1)}, bf16[1,104,384]{2,1,0:T(8,128)(2,1)S(1)}, u32[]{:S(2)}, u32[]{:S(2)}) collective-permute-start(bf16[1,104,384]{2,1,0:T(8,128)(2,1)S(1)} %collective-permute-done.11.refs_4_), channel_id=1, source_target_pairs={{0,1},{1,0},{2,3},{3,2},{4,5},{5,4},{6,7},{7,6},{8,9},{9,8},{10,11... | collective-permute-start | bytes 239624 | tf_op jit(solution)/shard_map/ppermute | solution.py:473
  53.6 6.8 %collective-permute-start.9 = (bf16[2,112,384]{2,1,0:T(8,128)(2,1)S(1)}, bf16[2,112,384]{2,1,0:T(8,128)(2,1)S(1)}, u32[]{:S(2)}, u32[]{:S(2)}) collective-permute-start(bf16[2,112,384]{2,1,0:T(8,128)(2,1)S(1)} %get-tuple-element.21), channel_id=1, source_target_pairs={{0,2},{2,0},{1,3},{3,1},{4,6},{6,4},{5,7},{7,5},{8,10},{10,8},{9,1... | collective-permute-start | bytes 516104 | tf_op jit(solution)/shard_map/ppermute | solution.py:473
  55.1 7.0 %collective-permute-start.13 = (bf16[4,112,384]{2,1,0:T(8,128)(2,1)S(1)}, bf16[4,112,384]{2,1,0:T(8,128)(2,1)S(1)}, u32[]{:S(2)}, u32[]{:S(2)}) collective-permute-start(bf16[4,112,384]{2,1,0:T(8,128)(2,1)S(1)} %get-tuple-element.22.refs_5_), channel_id=1, source_target_pairs={{0,1},{1,0},{2,3},{3,2},{4,5},{5,4},{6,7},{7,6},{8,9},{9,8},{10,11... | collective-permute-start | bytes 1032200 | tf_op jit(solution)/shard_map/ppermute | solution.py:473
  60.4 1.7 %collective-permute-start.10 = (bf16[2,112,384]{2,1,0:T(8,128)(2,1)S(1)}, bf16[2,112,384]{2,1,0:T(8,128)(2,1)S(1)}, u32[]{:S(2)}, u32[]{:S(2)}) collective-permute-start(bf16[2,112,384]{2,1,0:T(8,128)(2,1)S(1)} %collective-permute-done.9.refs_3_), channel_id=1, source_target_pairs={{0,1},{1,0},{2,3},{3,2},{4,5},{5,4},{6,7},{7,6},{8,9},{9,8},{10,11... | collective-permute-start | bytes 516104 | tf_op jit(solution)/shard_map/ppermute | solution.py:473

commit v2 on v1

--- a/solution.py
+++ b/solution.py
@@ -213,7 +213,7 @@
         return window[0] * ROWS + window[1]
 
 
-def bring_kernel(plan, tokens, qkv, mine, sem):
+def bring_kernel(plan, tokens, mine, sem):
     start = lax.axis_index("sub") * (plan.c * ROWS)
     copy = pltpu.make_async_copy(tokens.at[pl.ds(start, plan.c * ROWS)], mine, sem)
     copy.start()
@@ -506,9 +506,9 @@
         return jax.ShapeDtypeStruct(s, bf16)
 
     brought = call(
-        functools.partial(bring_kernel, plan), [HBM, VMEM], [shape(mine, T, d)],
+        functools.partial(bring_kernel, plan), [HBM], [shape(mine, T, d)],
         [pltpu.SemaphoreType.DMA], {}, 1_000_000, BRING, VMEM,
-    )(tokens, turned)[0]
+    )(tokens)[0]
     weights = (turned, w_out, other_qkv, other_out)
     slot = [
         pltpu.VMEM((2 * TP, d), bf16), pltpu.VMEM((2 * TP, 2 * d), bf16), pltpu.VMEM((2, d, TP), bf16),

time: 64.1 us -> 63.8 us (level)
  local copies, waits for them, and re-layouts: 1.18 us -> 0.01 us
  waiting for transfers between devices: 11.7 us -> 12.6 us
    unnamed x8, local copies, waits for them, and re-layouts: 1.18 us -> 0.01 us
    ppermute x10, waiting for transfers between devices: 5.06 us -> 5.99 us  [ring(): return lax.ppermute(value, tuple(axes), pairs)]
  transfers between devices with their start and end apart: 14 -> 14, of which waited for: 3 -> 4; matrix products, arithmetic and copies ran while one was open for 0% -> 0% of each run, Pallas kernels for 33% -> 33%
where the time goes in v2:
time: 63.8 us; the launch traced here: 63.7 us
  Pallas kernels  39.5 us (62%)
  waiting for transfers between devices  12.6 us (20%)
  starting transfers between devices  11.3 us (18%)
    pallas_call x2, Pallas kernels, first_call(): call(functools.partial(first_kernel, plan, which), [VMEM] * 7, outs, [plt...  17.9 us
    pallas_call x2, Pallas kernels, second_call(): call(functools.partial(second_kernel, plan, which, d), [VMEM] * len(ins),...  16.5 us
    ppermute x4, starting transfers between devices, beside(): lax.ppermute(value, axes, list(zip(line.ravel().tolist(), moved.ravel().t...  7.84 us
    ppermute x4, waiting for transfers between devices, beside(): lax.ppermute(value, axes, list(zip(line.ravel().tolist(), moved.ravel().t...  6.56 us
    ppermute x10, waiting for transfers between devices, ring(): return lax.ppermute(value, tuple(axes), pairs)  5.99 us
    ppermute x10, starting transfers between devices, ring(): return lax.ppermute(value, tuple(axes), pairs)  3.48 us
    pallas_call x2, Pallas kernels, place_call(): call(functools.partial(place_kernel, plan, which, d), [VMEM] * (len(ins)...  3.35 us
    pallas_call x1, Pallas kernels, shards(): call(functools.partial(bring_kernel, plan), [HBM], [shape(mine, T, d)], [...  1.7 us
  transfers between devices with their start and end apart: 14, of which 4 were waited for; matrix products, arithmetic and copies ran while one was open for 0% of the time, Pallas kernels for 33%

profile of v2, /device:TPU:0, one launch (start us, length us, event | category | flops | bytes accessed | tf_op | source)
XLA Modules:
  0.0 63.7 jit_solution(1248697686454963989)
XLA Ops:
  0.0 0.6 collective-permute-start
  0.6 0.1 collective-permute-start.1
  0.7 1.7 %shard_map.55.refs_0_ = bf16[16,200,384]{2,1,0:T(8,128)(2,1)S(1)} custom-call(bf16[32,200,384]{2,1,0:T(8,128)(2,1)} %tokens.1), custom_call_target="tpu_custom_call" | custom-call | flops 1000000 | bytes 4915200 | tf_op jit(solution)/shard_map/pallas_call | solution.py:508
  2.4 0.9 %collective-permute-done.1.refs_6_.refs_5_ = bf16[2,192,384]{2,1,0:T(8,128)(2,1)S(1)} collective-permute-done((bf16[2,192,384]{2,1,0:T(8,128)(2,1)}, bf16[2,192,384]{2,1,0:T(8,128)(2,1)S(1)}, u32[]{:S(2)}, u32[]{:S(2)}) %collective-permute-start.1) | collective-permute-done | bytes 294944 | tf_op jit(solution)/shard_map/ppermute | solution.py:473
  3.3 0.0 collective-permute-done.refs_5_.refs_4_
  3.3 9.0 %shard_map.56 = (bf16[8,224,384]{2,1,0:T(8,128)(2,1)S(1)}, bf16[4,224,384]{2,1,0:T(8,128)(2,1)S(1)}, bf16[3,128,384]{2,1,0:T(8,128)(2,1)S(1)}, bf16[1,128,384]{2,1,0:T(8,128)(2,1)S(1)}) custom-call(bf16[16,200,384]{2,1,0:T(8,128)(2,1)S(1)} %shard_map.55.refs_0_, s32[32,200]{1,0:T(8,128)S(1)} %copy-done.2, s32[1,128]{1,0:T(1,128)S(1)} %copy-done.3, ...), custom_call_target="tpu_custom_call" | custom-call | flops 96000000000 | bytes 4915200 | tf_op jit(solution)/shard_map/pallas_call | solution.py:522
  12.3 5.7 %collective-permute-start.4 = (bf16[1,128,384]{2,1,0:T(8,128)(2,1)S(1)}, bf16[1,128,384]{2,1,0:T(8,128)(2,1)S(1)}, u32[]{:S(2)}, u32[]{:S(2)}) collective-permute-start(bf16[1,128,384]{2,1,0:T(8,128)(2,1)S(1)} %get-tuple-element.17), channel_id=1, source_target_pairs={{0,15},{1,2},{4,3},{5,6},{8,7},{9,10},{12,11},{13,14},{2,13},{3,0}... | collective-permute-start | bytes 294920 | tf_op jit(solution)/shard_map/ppermute | solution.py:484
  18.0 0.5 collective-permute-start.3
  18.5 0.3 collective-permute-start.2
  18.8 8.9 %shard_map.57.refs_1_ = bf16[8,224,384]{2,1,0:T(8,128)(2,1)S(1)} custom-call(bf16[16,200,384]{2,1,0:T(8,128)(2,1)S(1)} %shard_map.55.refs_0_, s32[32,200]{1,0:T(8,128)S(1)} %copy-done.2, s32[1,128]{1,0:T(1,128)S(1)} %copy-done.3, bf16[2,3,192,384]{3,2,1,0:T(8,128)(2,1)S(1)} %bitcast.3, bf16[2,192,384]{2,1,0:T(8,128)(2,1)S(1)} %copy-done.1, ...), custom_call_target="tpu_custom_call" | custom-call | flops 96000000000 | bytes 2752512 | tf_op jit(solution)/shard_map/pallas_call | solution.py:522
  27.7 0.0 collective-permute-done.4.refs_8_
  27.8 7.5 %shard_map.58 = (bf16[8,200,384]{2,1,0:T(8,128)(2,1)S(1)}, bf16[4,200,384]{2,1,0:T(8,128)(2,1)S(1)}, bf16[2,112,384]{2,1,0:T(8,128)(2,1)S(1)}, bf16[1,104,384]{2,1,0:T(8,128)(2,1)S(1)}, bf16[4,112,384]{2,1,0:T(8,128)(2,1)S(1)}) custom-call(bf16[8,224,384]{2,1,0:T(8,128)(2,1)S(1)} %get-tuple-element.14.refs_0_, bf16[8,224,384]{2,1,0:T(8,128)(2,1)S(1)} %shard_map.57.refs_1_, ...), custom_call_target="tpu_custom_call" | custom-call | flops 96000000000 | bytes 4878336 | tf_op jit(solution)/shard_map/pallas_call | solution.py:542
  35.3 0.3 collective-permute-start.7
  35.6 0.1 collective-permute-start.5
  35.7 8.9 %shard_map.59.refs_1_ = bf16[8,200,384]{2,1,0:T(8,128)(2,1)S(1)} custom-call(bf16[8,224,384]{2,1,0:T(8,128)(2,1)S(1)} %get-tuple-element.14.refs_0_, bf16[8,224,384]{2,1,0:T(8,128)(2,1)S(1)} %shard_map.57.refs_1_, bf16[2,3,192,384]{3,2,1,0:T(8,128)(2,1)S(1)} %bitcast.5, bf16[2,192,384]{2,1,0:T(8,128)(2,1)S(1)} %copy-done.1, ...), custom_call_target="tpu_custom_call" | custom-call | flops 96000000000 | bytes 2457600 | tf_op jit(solution)/shard_map/pallas_call | solution.py:542
  44.6 0.5 collective-permute-start.6
  45.1 1.6 %collective-permute-done.7.refs_2_ = bf16[4,200,384]{2,1,0:T(8,128)(2,1)S(1)} collective-permute-done((bf16[4,200,384]{2,1,0:T(8,128)(2,1)S(1)}, bf16[4,200,384]{2,1,0:T(8,128)(2,1)S(1)}, u32[]{:S(2)}, u32[]{:S(2)}) %collective-permute-start.7) | collective-permute-done | bytes 614432 | tf_op jit(solution)/shard_map/ppermute | solution.py:484
  46.7 1.6 %collective-permute-start.11 = (bf16[1,104,384]{2,1,0:T(8,128)(2,1)S(1)}, bf16[1,104,384]{2,1,0:T(8,128)(2,1)S(1)}, u32[]{:S(2)}, u32[]{:S(2)}) collective-permute-start(bf16[1,104,384]{2,1,0:T(8,128)(2,1)S(1)} %get-tuple-element.19.refs_6_), channel_id=1, source_target_pairs={{0,3},{1,6},{4,7},{5,10},{8,11},{9,14},{12,15},{13,2},{2,1},{3,4},... | collective-permute-start | bytes 239624 | tf_op jit(solution)/shard_map/ppermute | solution.py:484
  48.3 4.9 %collective-permute-done.11.refs_4_ = bf16[1,104,384]{2,1,0:T(8,128)(2,1)S(1)} collective-permute-done((bf16[1,104,384]{2,1,0:T(8,128)(2,1)S(1)}, bf16[1,104,384]{2,1,0:T(8,128)(2,1)S(1)}, u32[]{:S(2)}, u32[]{:S(2)}) %collective-permute-start.11) | collective-permute-done | bytes 79904 | tf_op jit(solution)/shard_map/ppermute | solution.py:484
  53.3 1.5 %collective-permute-start.9 = (bf16[2,112,384]{2,1,0:T(8,128)(2,1)S(1)}, bf16[2,112,384]{2,1,0:T(8,128)(2,1)S(1)}, u32[]{:S(2)}, u32[]{:S(2)}) collective-permute-start(bf16[2,112,384]{2,1,0:T(8,128)(2,1)S(1)} %get-tuple-element.21), channel_id=1, source_target_pairs={{0,2},{2,0},{1,3},{3,1},{4,6},{6,4},{5,7},{7,5},{8,10},{10,8},{9,1... | collective-permute-start | bytes 516104 | tf_op jit(solution)/shard_map/ppermute | solution.py:473
  54.8 0.2 collective-permute-start.13
  55.0 5.1 %collective-permute-done.9.refs_3_ = bf16[2,112,384]{2,1,0:T(8,128)(2,1)S(1)} collective-permute-done((bf16[2,112,384]{2,1,0:T(8,128)(2,1)S(1)}, bf16[2,112,384]{2,1,0:T(8,128)(2,1)S(1)}, u32[]{:S(2)}, u32[]{:S(2)}) %collective-permute-start.9) | collective-permute-done | bytes 172064 | tf_op jit(solution)/shard_map/ppermute | solution.py:473
  60.1 1.7 %shard_map.60.refs_6_ = bf16[32,200,384]{2,1,0:T(8,128)(2,1)} custom-call(bf16[8,200,384]{2,1,0:T(8,128)(2,1)S(1)} %get-tuple-element.18.refs_0_, bf16[8,200,384]{2,1,0:T(8,128)(2,1)S(1)} %shard_map.59.refs_1_, bf16[4,200,384]{2,1,0:T(8,128)(2,1)S(1)} %collective-permute-done.7.refs_2_, bf16[2,112,384]{2,1,0:T(8,128)(2,1)S(1)} %collective-permute-done.9.refs_3_, ...), custom_call_target="tpu_custom_call" | custom-call | flops 100000000 | bytes 9830400 | tf_op jit(solution)/shard_map/pallas_call | solution.py:574
  61.8 1.7 %shard_map.61 = bf16[32,200,384]{2,1,0:T(8,128)(2,1)} custom-call(bf16[8,200,384]{2,1,0:T(8,128)(2,1)S(1)} %collective-permute-done.5.refs_0_, bf16[8,200,384]{2,1,0:T(8,128)(2,1)S(1)} %collective-permute-done.6.refs_1_, bf16[4,200,384]{2,1,0:T(8,128)(2,1)S(1)} %collective-permute-done.8.refs_2_, ...), custom_call_target="tpu_custom_call", output_to_operand_aliasing={{}: (6, {})} | custom-call | flops 100000000 | bytes 9830400 | tf_op jit(solution)/shard_map/pallas_call | solution.py:574
  (19 shorter events, 0.0 us)
Async XLA Ops:
  0.0 3.3 %copy-start = (bf16[2,3,384,192]{2,3,1,0:T(8,128)(2,1)S(1)}, bf16[2,3,384,192]{2,3,1,0:T(8,128)(2,1)}, u32[]{:S(2)}) copy-start(bf16[2,3,384,192]{2,3,1,0:T(8,128)(2,1)} %param.8) | copy-start | bytes 2654212
  0.0 3.3 %copy-start.1 = (bf16[2,192,384]{2,1,0:T(8,128)(2,1)S(1)}, bf16[2,192,384]{2,1,0:T(8,128)(2,1)}, u32[]{:S(2)}) copy-start(bf16[2,192,384]{2,1,0:T(8,128)(2,1)} %refs_3_.3) | copy-start | bytes 884740
  0.0 3.3 %copy-start.2 = (s32[32,200]{1,0:T(8,128)S(1)}, s32[32,200]{1,0:T(8,128)}, u32[]{:S(2)}) copy-start(s32[32,200]{1,0:T(8,128)} %refs_1_.3) | copy-start | bytes 76804
  0.0 3.3 %copy-start.3 = (s32[1,128]{1,0:T(1,128)S(1)}, s32[1,128]{1,0:T(1,128)}, u32[]{:S(2)}) copy-start(s32[1,128]{1,0:T(1,128)} %refs_2_.3) | copy-start | bytes 1540
  0.0 3.3 %collective-permute-start = (bf16[2,3,192,384]{3,2,1,0:T(8,128)(2,1)}, bf16[2,3,192,384]{3,2,1,0:T(8,128)(2,1)S(1)}, u32[]{:S(2)}, u32[]{:S(2)}) collective-permute-start(bf16[2,3,192,384]{3,2,1,0:T(8,128)(2,1)} %bitcast.1), channel_id=1, source_target_pairs={{0,1},{1,0},{2,3},{3,2},{4,5},{5,4},{6,7},{7,6},{8,9},{9,8},{10,11... | collective-permute-start | bytes 2654216 | tf_op jit(solution)/shard_map/ppermute | solution.py:473
  0.6 2.7 %collective-permute-start.1 = (bf16[2,192,384]{2,1,0:T(8,128)(2,1)}, bf16[2,192,384]{2,1,0:T(8,128)(2,1)S(1)}, u32[]{:S(2)}, u32[]{:S(2)}) collective-permute-start(bf16[2,192,384]{2,1,0:T(8,128)(2,1)} %refs_3_.3), channel_id=1, source_target_pairs={{0,1},{1,0},{2,3},{3,2},{4,5},{5,4},{6,7},{7,6},{8,9},{9,8},{10,11... | collective-permute-start | bytes 884744 | tf_op jit(solution)/shard_map/ppermute | solution.py:473
  12.3 15.4 %collective-permute-start.4 = (bf16[1,128,384]{2,1,0:T(8,128)(2,1)S(1)}, bf16[1,128,384]{2,1,0:T(8,128)(2,1)S(1)}, u32[]{:S(2)}, u32[]{:S(2)}) collective-permute-start(bf16[1,128,384]{2,1,0:T(8,128)(2,1)S(1)} %get-tuple-element.17), channel_id=1, source_target_pairs={{0,15},{1,2},{4,3},{5,6},{8,7},{9,10},{12,11},{13,14},{2,13},{3,0}... | collective-permute-start | bytes 294920 | tf_op jit(solution)/shard_map/ppermute | solution.py:484
  18.0 9.8 %collective-permute-start.3 = (bf16[3,128,384]{2,1,0:T(8,128)(2,1)S(1)}, bf16[3,128,384]{2,1,0:T(8,128)(2,1)S(1)}, u32[]{:S(2)}, u32[]{:S(2)}) collective-permute-start(bf16[3,128,384]{2,1,0:T(8,128)(2,1)S(1)} %get-tuple-element.16), channel_id=1, source_target_pairs={{0,2},{2,0},{1,3},{3,1},{4,6},{6,4},{5,7},{7,5},{8,10},{10,8},{9,1... | collective-permute-start | bytes 884744 | tf_op jit(solution)/shard_map/ppermute | solution.py:473
  18.5 9.2 %collective-permute-start.2 = (bf16[4,224,384]{2,1,0:T(8,128)(2,1)S(1)}, bf16[4,224,384]{2,1,0:T(8,128)(2,1)S(1)}, u32[]{:S(2)}, u32[]{:S(2)}) collective-permute-start(bf16[4,224,384]{2,1,0:T(8,128)(2,1)S(1)} %get-tuple-element.15), channel_id=1, source_target_pairs={{0,13},{1,0},{4,1},{5,4},{8,5},{9,8},{12,9},{13,12},{2,15},{3,2},{... | collective-permute-start | bytes 2064392 | tf_op jit(solution)/shard_map/ppermute | solution.py:484
  35.3 11.4 %collective-permute-start.7 = (bf16[4,200,384]{2,1,0:T(8,128)(2,1)S(1)}, bf16[4,200,384]{2,1,0:T(8,128)(2,1)S(1)}, u32[]{:S(2)}, u32[]{:S(2)}) collective-permute-start(bf16[4,200,384]{2,1,0:T(8,128)(2,1)S(1)} %get-tuple-element.20), channel_id=1, source_target_pairs={{0,1},{1,4},{4,5},{5,8},{8,9},{9,12},{12,13},{13,0},{2,3},{3,6},{6... | collective-permute-start | bytes 1843208 | tf_op jit(solution)/shard_map/ppermute | solution.py:484
  35.6 26.2 %collective-permute-start.5 = (bf16[8,200,384]{2,1,0:T(8,128)(2,1)S(1)}, bf16[8,200,384]{2,1,0:T(8,128)(2,1)S(1)}, u32[]{:S(2)}, u32[]{:S(2)}) collective-permute-start(bf16[8,200,384]{2,1,0:T(8,128)(2,1)S(1)} %get-tuple-element.18.refs_0_), channel_id=1, source_target_pairs={{0,1},{1,0},{2,3},{3,2},{4,5},{5,4},{6,7},{7,6},{8,9},{9,8},{10,11... | collective-permute-start | bytes 3686408 | tf_op jit(solution)/shard_map/ppermute | solution.py:473
  44.6 17.2 %collective-permute-start.6 = (bf16[8,200,384]{2,1,0:T(8,128)(2,1)S(1)}, bf16[8,200,384]{2,1,0:T(8,128)(2,1)S(1)}, u32[]{:S(2)}, u32[]{:S(2)}) collective-permute-start(bf16[8,200,384]{2,1,0:T(8,128)(2,1)S(1)} %shard_map.59.refs_1_), channel_id=1, source_target_pairs={{0,1},{1,0},{2,3},{3,2},{4,5},{5,4},{6,7},{7,6},{8,9},{9,8},{10,11... | collective-permute-start | bytes 3686408 | tf_op jit(solution)/shard_map/ppermute | solution.py:473
  46.7 15.0 %collective-permute-start.8 = (bf16[4,200,384]{2,1,0:T(8,128)(2,1)S(1)}, bf16[4,200,384]{2,1,0:T(8,128)(2,1)S(1)}, u32[]{:S(2)}, u32[]{:S(2)}) collective-permute-start(bf16[4,200,384]{2,1,0:T(8,128)(2,1)S(1)} %collective-permute-done.7.refs_2_), channel_id=1, source_target_pairs={{0,1},{1,0},{2,3},{3,2},{4,5},{5,4},{6,7},{7,6},{8,9},{9,8},{10,11... | collective-permute-start | bytes 1843208 | tf_op jit(solution)/shard_map/ppermute | solution.py:473
  46.7 6.5 %collective-permute-start.11 = (bf16[1,104,384]{2,1,0:T(8,128)(2,1)S(1)}, bf16[1,104,384]{2,1,0:T(8,128)(2,1)S(1)}, u32[]{:S(2)}, u32[]{:S(2)}) collective-permute-start(bf16[1,104,384]{2,1,0:T(8,128)(2,1)S(1)} %get-tuple-element.19.refs_6_), channel_id=1, source_target_pairs={{0,3},{1,6},{4,7},{5,10},{8,11},{9,14},{12,15},{13,2},{2,1},{3,4},... | collective-permute-start | bytes 239624 | tf_op jit(solution)/shard_map/ppermute | solution.py:484
  53.3 1.5 %collective-permute-start.12 = (bf16[1,104,384]{2,1,0:T(8,128)(2,1)S(1)}, bf16[1,104,384]{2,1,0:T(8,128)(2,1)S(1)}, u32[]{:S(2)}, u32[]{:S(2)}) collective-permute-start(bf16[1,104,384]{2,1,0:T(8,128)(2,1)S(1)} %collective-permute-done.11.refs_4_), channel_id=1, source_target_pairs={{0,1},{1,0},{2,3},{3,2},{4,5},{5,4},{6,7},{7,6},{8,9},{9,8},{10,11... | collective-permute-start | bytes 239624 | tf_op jit(solution)/shard_map/ppermute | solution.py:473
  53.3 6.8 %collective-permute-start.9 = (bf16[2,112,384]{2,1,0:T(8,128)(2,1)S(1)}, bf16[2,112,384]{2,1,0:T(8,128)(2,1)S(1)}, u32[]{:S(2)}, u32[]{:S(2)}) collective-permute-start(bf16[2,112,384]{2,1,0:T(8,128)(2,1)S(1)} %get-tuple-element.21), channel_id=1, source_target_pairs={{0,2},{2,0},{1,3},{3,1},{4,6},{6,4},{5,7},{7,5},{8,10},{10,8},{9,1... | collective-permute-start | bytes 516104 | tf_op jit(solution)/shard_map/ppermute | solution.py:473
  54.8 7.0 %collective-permute-start.13 = (bf16[4,112,384]{2,1,0:T(8,128)(2,1)S(1)}, bf16[4,112,384]{2,1,0:T(8,128)(2,1)S(1)}, u32[]{:S(2)}, u32[]{:S(2)}) collective-permute-start(bf16[4,112,384]{2,1,0:T(8,128)(2,1)S(1)} %get-tuple-element.22.refs_5_), channel_id=1, source_target_pairs={{0,1},{1,0},{2,3},{3,2},{4,5},{5,4},{6,7},{7,6},{8,9},{9,8},{10,11... | collective-permute-start | bytes 1032200 | tf_op jit(solution)/shard_map/ppermute | solution.py:473
  60.1 1.7 %collective-permute-start.10 = (bf16[2,112,384]{2,1,0:T(8,128)(2,1)S(1)}, bf16[2,112,384]{2,1,0:T(8,128)(2,1)S(1)}, u32[]{:S(2)}, u32[]{:S(2)}) collective-permute-start(bf16[2,112,384]{2,1,0:T(8,128)(2,1)S(1)} %collective-permute-done.9.refs_3_), channel_id=1, source_target_pairs={{0,1},{1,0},{2,3},{3,2},{4,5},{5,4},{6,7},{7,6},{8,9},{9,8},{10,11... | collective-permute-start | bytes 516104 | tf_op jit(solution)/shard_map/ppermute | solution.py:473
